TPU v7x, 32 devices: a whole 2x2x4 slice. The times are simulated.
32 devices in a mesh: seq: 4 (over x, core), head: 8 (over z, y).
Axes of the slice: x: 2, y: 2, z: 4, core: 2. Of those that a mesh axis runs over, the one named last changes fastest.
Arguments:
- inner_input: bfloat16 [2048, 16384], P('seq', 'head'), may hold values from -6 to 6
- gate_input: bfloat16 [2048, 16384], P('seq', 'head'), may hold values from -48 to 48
- bc_input: bfloat16 [2048, 4096], P('seq'), may hold values from -6 to 6
- dt_input: float32 [256, 2048], P('head', 'seq'), may hold values from -11.5 to 0
- log_rate: float32 [256], P('head'), may hold values from -1.2 to 0
- skip_weight: float32 [256], P('head'), may hold values from 0.5 to 1.5
- conv_weight_x: float32 [4, 16384], P(None, 'head'), may hold values from -3 to 3
- conv_bias_x: float32 [16384], P('head'), may hold values from -3 to 3
- conv_weight_bc: float32 [4, 4096], replicated, may hold values from -3 to 3
- conv_bias_bc: float32 [4096], replicated, may hold values from -3 to 3
- conv_tail_x: bfloat16 [3, 16384], P(None, 'head'), may hold values from -6 to 6
- conv_tail_bc: bfloat16 [3, 4096], replicated, may hold values from -6 to 6
- init_state: float32 [256, 64, 256], P('head'), may hold values from -0.6 to 0.6
- norm_gain: float32 [16384], P('head'), may hold values from 0.5 to 1.5
- out_weight: bfloat16 [16384, 8192], P('head', 'seq'), may hold values from -0.046875 to 0.046875
Outputs:
- layer_out: bfloat16 [2048, 8192], P(('seq', 'head'))
- boundary_states: float32 [4, 256, 64, 256], P('seq', 'head')
All inputs are finite; a program needn't handle non-finite values.
Results may differ from a plain program's by a relative error of at most 0.015.
Values may be sent and summed in bfloat16 or wider, within the bound.
A program may use at most 192 MiB of HBM per device.

v0:
```python
import jax
import jax.numpy as jnp
from jax import lax
from jax.sharding import PartitionSpec as P

MIXER_HEADS = 256
HEADDIM = 64
STATE = 256
GROUPS = 8
KERNEL = 4
SPAN = 128
DINNER = 16384
highest = lax.Precision.HIGHEST
norm_eps = 1e-05


def from_behind(x, axis, by):
    count = lax.axis_size(axis)
    pairs = [(i, i + by) for i in range(count) if 0 <= i + by < count]
    return lax.ppermute(x, axis, pairs)


def carried_in(x, axis, join, neutral):
    place = lax.axis_index(axis)
    gathered = jax.tree.map(
        lambda a, kind: lax.all_gather(a.astype(kind), axis), x, (jnp.bfloat16, jnp.bfloat16)
    )
    state = jax.tree.map(lambda a, e: jnp.zeros_like(a) + jnp.asarray(e, a.dtype), x, neutral)

    def one(lap, state):
        return join(
            state,
            jax.tree.map(
                lambda a, own: lax.dynamic_index_in_dim(a, lap, 0, False).astype(own.dtype),
                gathered,
                x,
            ),
        )

    return lax.fori_loop(0, place, one, state)


def causal_conv(values, previous, kernel_weight, kernel_bias):
    extended = jnp.concatenate([previous, values], axis=0)
    length = values.shape[0]
    running = jnp.zeros_like(values) + kernel_bias[None, :]
    for offset in range(KERNEL):
        running = running + kernel_weight[offset][None, :] * extended[offset : offset + length]
    return running


def ssd_block(span_x, span_b, span_c, span_step, span_log, state):
    cumul = jnp.cumsum(span_log, axis=1)
    length = span_x.shape[0]
    causal = (jnp.arange(length)[:, None] >= jnp.arange(length)[None, :])[None]
    spread = jnp.where(causal, cumul[:, :, None] - cumul[:, None, :], 0.0)
    decays = jnp.where(causal, jnp.exp(spread), 0.0)
    scores = jnp.einsum("thn,shn->hts", span_c, span_b, precision=highest)
    mixer = scores * decays * span_step[:, None, :]
    output = jnp.einsum("hts,shp->thp", mixer, span_x, precision=highest)
    carried = jnp.einsum("thn,hpn->thp", span_c, state, precision=highest)
    output = output + jnp.exp(cumul).T[:, :, None] * carried
    weights = jnp.exp(cumul[:, -1:] - cumul) * span_step
    written = jnp.einsum("hs,shp,shn->hpn", weights, span_x, span_b, precision=highest)
    new_state = jnp.exp(cumul[:, -1])[:, None, None] * state + written
    return (output, new_state)


def body(
    inner_input,
    gate_input,
    bc_input,
    dt_input,
    log_rate,
    skip_weight,
    conv_weight_x,
    conv_bias_x,
    conv_weight_bc,
    conv_bias_bc,
    conv_tail_x,
    conv_tail_bc,
    init_state,
    norm_gain,
    out_weight,
):
    seq_index = lax.axis_index("seq")
    head_index = lax.axis_index("head")
    row_count = inner_input.shape[0]
    channels = inner_input.shape[1]
    heads_here = dt_input.shape[0]
    per_group = MIXER_HEADS // GROUPS
    heads_shared = min(heads_here, per_group)
    groups_here = heads_here // heads_shared
    group_first = head_index * heads_here // per_group
    width_bc = groups_here * STATE

    def own_columns(table, table_dim):
        part_b = lax.dynamic_slice_in_dim(table, group_first * STATE, width_bc, table_dim)
        part_c = lax.dynamic_slice_in_dim(
            table, GROUPS * STATE + group_first * STATE, width_bc, table_dim
        )
        return jnp.concatenate([part_b, part_c], axis=table_dim)

    own_bc = own_columns(bc_input, 1)
    tail_rows = row_count - KERNEL + 1
    arrived = from_behind((inner_input[tail_rows:], own_bc[tail_rows:]), "seq", 1)
    at_first = seq_index == 0
    previous_x = jnp.where(at_first, conv_tail_x, arrived[0])
    previous_bc = jnp.where(at_first, own_columns(conv_tail_bc, 1), arrived[1])
    conv_x = jax.nn.silu(
        causal_conv(
            inner_input.astype(jnp.float32),
            previous_x.astype(jnp.float32),
            conv_weight_x,
            conv_bias_x,
        )
    ).astype(jnp.bfloat16)
    conv_bc = jax.nn.silu(
        causal_conv(
            own_bc.astype(jnp.float32),
            previous_bc.astype(jnp.float32),
            own_columns(conv_weight_bc, 1),
            own_columns(conv_bias_bc, 0),
        )
    ).astype(jnp.bfloat16)
    stride_length = jax.nn.softplus(dt_input)
    decay_log = -jnp.exp(log_rate)[:, None] * stride_length
    spans_here = row_count // SPAN
    all_x = conv_x.astype(jnp.float32).reshape(row_count, heads_here, HEADDIM)
    bc_float = conv_bc.astype(jnp.float32)
    all_b = jnp.repeat(
        bc_float[:, :width_bc].reshape(row_count, groups_here, STATE), heads_shared, axis=1
    )
    all_c = jnp.repeat(
        bc_float[:, width_bc:].reshape(row_count, groups_here, STATE), heads_shared, axis=1
    )

    def span_step_body(state, span_index):
        first_row = span_index * SPAN
        span_x = lax.dynamic_slice_in_dim(all_x, first_row, SPAN, 0)
        span_b = lax.dynamic_slice_in_dim(all_b, first_row, SPAN, 0)
        span_c = lax.dynamic_slice_in_dim(all_c, first_row, SPAN, 0)
        span_step = lax.dynamic_slice_in_dim(stride_length, first_row, SPAN, 1)
        span_log = lax.dynamic_slice_in_dim(decay_log, first_row, SPAN, 1)
        output, new_state = ssd_block(span_x, span_b, span_c, span_step, span_log, state)
        return (new_state, output)

    empty_state = jnp.zeros((heads_here, HEADDIM, STATE), jnp.float32)
    local_state, local_out = lax.scan(
        span_step_body, empty_state, jnp.arange(spans_here, dtype=jnp.int32)
    )
    local_out = local_out.reshape(row_count, heads_here, HEADDIM)
    cumul = jnp.cumsum(decay_log, axis=1)
    total_log = cumul[:, -1]

    def combine(earlier, later):
        return (earlier[0] + later[0], jnp.exp(later[0])[:, None, None] * earlier[1] + later[1])

    identity = (jnp.zeros((heads_here,), jnp.float32), empty_state)
    prior_log, prior_state = carried_in((total_log, local_state), "seq", combine, identity)
    incoming = jnp.exp(prior_log)[:, None, None] * init_state + prior_state
    incoming_term = jnp.einsum("thn,hpn->thp", all_c, incoming, precision=highest)
    outputs = (
        local_out
        + jnp.exp(cumul).T[:, :, None] * incoming_term
        + skip_weight[None, :, None] * all_x
    )
    boundary = (jnp.exp(total_log)[:, None, None] * incoming + local_state)[None]
    mixed = outputs.reshape(row_count, channels) * jax.nn.silu(gate_input.astype(jnp.float32))
    group_width = DINNER // GROUPS
    piece_width = min(channels, group_width)
    pieces_here = channels // piece_width
    pieces = mixed.reshape(row_count, pieces_here, piece_width)
    squares = jnp.sum(pieces * pieces, axis=2).T
    own_group = (head_index * pieces_here + jnp.arange(pieces_here)) * piece_width // group_width
    membership = (own_group[:, None] == jnp.arange(GROUPS)[None, :]).astype(jnp.float32)
    contribution = jnp.dot(membership.T, squares, precision=highest)
    group_totals = lax.psum(contribution, "head")
    group_sums = jnp.dot(membership, group_totals, precision=highest)
    inverse_rms = lax.rsqrt(group_sums / group_width + norm_eps).T
    normed = (
        (pieces * inverse_rms[:, :, None]).reshape(row_count, channels) * norm_gain[None, :]
    ).astype(jnp.bfloat16)
    terms = jnp.dot(
        normed,
        lax.all_gather(out_weight, "seq", axis=1, tiled=True),
        preferred_element_type=jnp.float32,
    )
    layer_out = lax.psum_scatter(
        terms.astype(jnp.bfloat16), "head", scatter_dimension=0, tiled=True
    )
    return (layer_out, boundary)


def solution(mesh):
    in_specs = (
        P("seq", "head"),
        P("seq", "head"),
        P("seq", None),
        P("head", "seq"),
        P("head"),
        P("head"),
        P(None, "head"),
        P("head"),
        P(),
        P(),
        P(None, "head"),
        P(),
        P("head", None, None),
        P("head"),
        P("head", "seq"),
    )
    out_specs = (P(("seq", "head"), None), P("seq", "head", None, None))
    return jax.shard_map(body, mesh=mesh, in_specs=in_specs, out_specs=out_specs, check_vma=False)
```

profile of v0, /device:TPU:0, one launch (start us, length us, event | category | flops | bytes accessed | tf_op | source)
XLA Modules:
  0.0 697.1 jit_solution(13256864626759303394)
XLA Ops:
  35.2 7.6 %reshape.131 = f32[512,32,256]{2,0,1:T(8,128)} broadcast(f32[512,256]{1,0:T(8,128)S(1)} %get-tuple-element.156), dimensions={0,2} | broadcast | bytes 17301504 | tf_op jit(solution)/shard_map/reshape | solution.py:131
  42.9 7.6 %reshape.132 = f32[512,32,256]{2,0,1:T(8,128)} broadcast(f32[512,256]{1,0:T(8,128)S(1)} %get-tuple-element.155), dimensions={0,2} | broadcast | bytes 17301504 | tf_op jit(solution)/shard_map/reshape | solution.py:134
  50.5 222.8 %while.26 = (s32[]{:T(128)}, f32[32,64,256]{2,1,0:T(8,128)S(1)}, f32[4,128,32,64]{1,0,3,2:T(4,128)}, s32[4]{0:T(128)S(1)}, f32[32,512]{1,0:T(8,128)S(1)}, /*inde...) while((s32[]{:T(128)}, f32[32,64,256]{2,1,0:T(8,128)S(1)}, ...), condition=%wide.region_2.3_spmd.clone, body=%wide.region_0.2_spmd.clone.sunk | while | flops 3629928448 | bytes 34868704 | solution.py:149
  52.3 7.9 %fusion.122 = f32[32,128,128]{2,1,0:T(8,128)S(1)} fusion(f32[512,32,256]{2,0,1:T(8,128)} %get-tuple-element.312, s32[]{:T(128)S(6)} %select_n.102, f32[512,32,256]{2,0,1:T(8,128)} %get-tuple-element.311), kind=kOutput, calls=%fused_computation.6.clone.1 | convolution fusion | flops 1610612736 | bytes 10486784 | tf_op jit(solution)/shard_map/while/body/eval_jaxpr/thn,shn->hts/dot_general | solution.py:58
  66.7 7.3 %fusion.124 = f32[128,32,64]{0,2,1:T(8,128)S(1)} fusion(f32[128,32,64]{0,2,1:T(8,128)} %fusion.123, f32[32,64,256]{2,1,0:T(8,128)S(1)} %get-tuple-element.291, f32[512,32,256]{2,0,1:T(8,128)} %get-tuple-element.312, s32[]{:T(128)S(6)} %select_n.102, pred[]{:T(512)S(6)} %compare.7, f32[128,32]{0,1:T(8,128)S(1)} %get-tuple-element.275), kind=kOutput, calls=%fused_computation.23.clone.1 | convolution fusion | flops 806354944 | bytes 8404997 | tf_op jit(solution)/shard_map/while/body/eval_jaxpr/thn,hpn->thp/dot_general | solution.py:61
  74.0 26.4 %dynamic_update_slice.6 = f32[4,128,32,64]{1,0,3,2:T(4,128)} dynamic-update-slice(f32[4,128,32,64]{1,0,3,2:T(4,128)} %get-tuple-element.292, f32[1,128,32,64]{1,0,3,2:T(1,128)S(1)} %bitcast.82, s32[]{:T(128)} %get-tuple-element.290, s32[]{:T(128)} %constant.87.clone.1..sunk.1, s32[]{:T(128)} %constant.87.clone.1..sunk.1, s32[]{:T(128)} %constant.87.clone.1..sunk.1) | dynamic-update-slice | bytes 2097156 | tf_op jit(solution)/shard_map/while/body/jit(dynamic_update_index_in_dim)/dynamic_update_slice | solution.py:149
  107.9 7.9 %fusion.122 = f32[32,128,128]{2,1,0:T(8,128)S(1)} fusion(f32[512,32,256]{2,0,1:T(8,128)} %get-tuple-element.312, s32[]{:T(128)S(6)} %select_n.102, f32[512,32,256]{2,0,1:T(8,128)} %get-tuple-element.311), kind=kOutput, calls=%fused_computation.6.clone.1 | convolution fusion | flops 1610612736 | bytes 10486784 | tf_op jit(solution)/shard_map/while/body/eval_jaxpr/thn,shn->hts/dot_general | solution.py:58
  115.8 6.5 fusion.123
  122.3 7.3 %fusion.124 = f32[128,32,64]{0,2,1:T(8,128)S(1)} fusion(f32[128,32,64]{0,2,1:T(8,128)} %fusion.123, f32[32,64,256]{2,1,0:T(8,128)S(1)} %get-tuple-element.291, f32[512,32,256]{2,0,1:T(8,128)} %get-tuple-element.312, s32[]{:T(128)S(6)} %select_n.102, pred[]{:T(512)S(6)} %compare.7, f32[128,32]{0,1:T(8,128)S(1)} %get-tuple-element.275), kind=kOutput, calls=%fused_computation.23.clone.1 | convolution fusion | flops 806354944 | bytes 8404997 | tf_op jit(solution)/shard_map/while/body/eval_jaxpr/thn,hpn->thp/dot_general | solution.py:61
  129.6 26.4 %dynamic_update_slice.6 = f32[4,128,32,64]{1,0,3,2:T(4,128)} dynamic-update-slice(f32[4,128,32,64]{1,0,3,2:T(4,128)} %get-tuple-element.292, f32[1,128,32,64]{1,0,3,2:T(1,128)S(1)} %bitcast.82, s32[]{:T(128)} %get-tuple-element.290, s32[]{:T(128)} %constant.87.clone.1..sunk.1, s32[]{:T(128)} %constant.87.clone.1..sunk.1, s32[]{:T(128)} %constant.87.clone.1..sunk.1) | dynamic-update-slice | bytes 2097156 | tf_op jit(solution)/shard_map/while/body/jit(dynamic_update_index_in_dim)/dynamic_update_slice | solution.py:149
  163.5 7.9 %fusion.122 = f32[32,128,128]{2,1,0:T(8,128)S(1)} fusion(f32[512,32,256]{2,0,1:T(8,128)} %get-tuple-element.312, s32[]{:T(128)S(6)} %select_n.102, f32[512,32,256]{2,0,1:T(8,128)} %get-tuple-element.311), kind=kOutput, calls=%fused_computation.6.clone.1 | convolution fusion | flops 1610612736 | bytes 10486784 | tf_op jit(solution)/shard_map/while/body/eval_jaxpr/thn,shn->hts/dot_general | solution.py:58
  171.5 6.5 fusion.123
  178.0 7.3 %fusion.124 = f32[128,32,64]{0,2,1:T(8,128)S(1)} fusion(f32[128,32,64]{0,2,1:T(8,128)} %fusion.123, f32[32,64,256]{2,1,0:T(8,128)S(1)} %get-tuple-element.291, f32[512,32,256]{2,0,1:T(8,128)} %get-tuple-element.312, s32[]{:T(128)S(6)} %select_n.102, pred[]{:T(512)S(6)} %compare.7, f32[128,32]{0,1:T(8,128)S(1)} %get-tuple-element.275), kind=kOutput, calls=%fused_computation.23.clone.1 | convolution fusion | flops 806354944 | bytes 8404997 | tf_op jit(solution)/shard_map/while/body/eval_jaxpr/thn,hpn->thp/dot_general | solution.py:61
  185.2 26.4 %dynamic_update_slice.6 = f32[4,128,32,64]{1,0,3,2:T(4,128)} dynamic-update-slice(f32[4,128,32,64]{1,0,3,2:T(4,128)} %get-tuple-element.292, f32[1,128,32,64]{1,0,3,2:T(1,128)S(1)} %bitcast.82, s32[]{:T(128)} %get-tuple-element.290, s32[]{:T(128)} %constant.87.clone.1..sunk.1, s32[]{:T(128)} %constant.87.clone.1..sunk.1, s32[]{:T(128)} %constant.87.clone.1..sunk.1) | dynamic-update-slice | bytes 2097156 | tf_op jit(solution)/shard_map/while/body/jit(dynamic_update_index_in_dim)/dynamic_update_slice | solution.py:149
  219.2 7.9 %fusion.122 = f32[32,128,128]{2,1,0:T(8,128)S(1)} fusion(f32[512,32,256]{2,0,1:T(8,128)} %get-tuple-element.312, s32[]{:T(128)S(6)} %select_n.102, f32[512,32,256]{2,0,1:T(8,128)} %get-tuple-element.311), kind=kOutput, calls=%fused_computation.6.clone.1 | convolution fusion | flops 1610612736 | bytes 10486784 | tf_op jit(solution)/shard_map/while/body/eval_jaxpr/thn,shn->hts/dot_general | solution.py:58
  227.1 6.5 fusion.123
  233.6 7.3 %fusion.124 = f32[128,32,64]{0,2,1:T(8,128)S(1)} fusion(f32[128,32,64]{0,2,1:T(8,128)} %fusion.123, f32[32,64,256]{2,1,0:T(8,128)S(1)} %get-tuple-element.291, f32[512,32,256]{2,0,1:T(8,128)} %get-tuple-element.312, s32[]{:T(128)S(6)} %select_n.102, pred[]{:T(512)S(6)} %compare.7, f32[128,32]{0,1:T(8,128)S(1)} %get-tuple-element.275), kind=kOutput, calls=%fused_computation.23.clone.1 | convolution fusion | flops 806354944 | bytes 8404997 | tf_op jit(solution)/shard_map/while/body/eval_jaxpr/thn,hpn->thp/dot_general | solution.py:61
  240.9 26.4 %dynamic_update_slice.6 = f32[4,128,32,64]{1,0,3,2:T(4,128)} dynamic-update-slice(f32[4,128,32,64]{1,0,3,2:T(4,128)} %get-tuple-element.292, f32[1,128,32,64]{1,0,3,2:T(1,128)S(1)} %bitcast.82, s32[]{:T(128)} %get-tuple-element.290, s32[]{:T(128)} %constant.87.clone.1..sunk.1, s32[]{:T(128)} %constant.87.clone.1..sunk.1, s32[]{:T(128)} %constant.87.clone.1..sunk.1) | dynamic-update-slice | bytes 2097156 | tf_op jit(solution)/shard_map/while/body/jit(dynamic_update_index_in_dim)/dynamic_update_slice | solution.py:149
  289.8 19.6 %all-gather.7.cloned.1.call-done = bf16[128,64,256]{2,1,0:T(8,128)(2,1)} async-done(((bf16[32,64,256]{2,1,0:T(8,128)(2,1)}), bf16[128,64,256]{2,1,0:T(8,128)(2,1)}) %all-gather.7.cloned.1.call-update) | async-done | bytes 4194320 | tf_op jit(solution)/shard_map/all_gather | solution.py:26
  311.9 20.5 %fusion.68 = f32[512,32,64]{0,2,1:T(8,128)} fusion(f32[512,32,64]{0,2,1:T(8,128)} %reshape.133, f32[512,32,64]{0,2,1:T(8,128)} %get-tuple-element.348, f32[512,256]{1,0:T(8,128)S(1)} %copy-done.2, f32[32]{0:T(128)S(1)} %copy-done.6, f32[512,32]{0,1:T(8,128)S(1)} %exponential_bitcast_fusion.1, f32[32,64,256]{2,1,0:T(8,128)} %get-tuple-element.87, ...), kind=kOutput, calls=%fused_computation.70 | convolution fusion | flops 3226468352 | bytes 17367296 | tf_op jit(solution)/shard_map/thn,hpn->thp/dot_general | solution.py:162
  343.1 37.3 %psum.7 = f32[8,512]{1,0:T(8,128)S(1)} all-reduce(f32[8,512]{1,0:T(8,128)S(1)} %broadcast_multiply_fusion.1), channel_id=1, replica_groups=mesh['seq'=4,'head'=8] {'head'}, use_global_device_ids=true, to_apply=%region_8.9 | all-reduce | flops 4096 | bytes 32768 | tf_op jit(solution)/shard_map/psum | solution.py:178
  380.5 132.0 %all-gather.5.cloned.1.call-done = bf16[2048,8192]{1,0:T(8,128)(2,1)} async-done(((bf16[2048,2048]{1,0:T(8,128)(2,1)}), bf16[2048,8192]{1,0:T(8,128)(2,1)}) %all-gather.5.cloned.1.call-update) | async-done | bytes 33554448 | tf_op jit(solution)/shard_map/all_gather | solution.py:186
  512.5 28.9 %convolution_convert_fusion = bf16[512,8192]{1,0:T(8,128)(2,1)} fusion(bf16[2048,8192]{1,0:T(8,128)(2,1)} %all-gather.5.cloned.1.call-done, f32[2048]{0:T(1024)S(1)} %copy-done.7, f32[512]{0:T(512)S(1)} %add_rsqrt_fusion, f32[512,2048]{1,0:T(8,128)} %copy.36, bf16[512,2048]{1,0:T(8,128)(2,1)} %param.20), kind=kOutput, calls=%fused_computation.47 | convolution fusion | flops 17193500672 | bytes 48244736 | tf_op jit(solution)/shard_map/dot_general | solution.py:184
  545.6 145.0 %reduce-scatter.2.cloned.1.call-done = bf16[64,8192]{1,0:T(8,128)(2,1)} async-done(((bf16[512,8192]{1,0:T(8,128)(2,1)}), bf16[64,8192]{1,0:T(8,128)(2,1)}) %reduce-scatter.2.cloned.1.call-update) | async-done | bytes 1048592 | tf_op jit(solution)/shard_map/reduce_scatter | solution.py:189
  (110 shorter events, 95.3 us)
Async XLA Ops:
  7.2 302.2 %all-gather.7.cloned.1.call-start = ((), (), s32[]{:S(2)}) async-start(), calls=%async_computation.3 | async-start | bytes 5242880 | tf_op jit(solution)/shard_map/all_gather | solution.py:26
  7.2 13.8 %copy-start.3 = (bf16[512,2048]{1,0:T(8,128)(2,1)S(1)}, bf16[512,2048]{1,0:T(8,128)(2,1)}, u32[]{:S(2)}) copy-start(bf16[512,2048]{1,0:T(8,128)(2,1)} %param.19) | copy-start | bytes 6291460
  8.5 15.0 %collective-permute-start.1 = (bf16[3,512]{1,0:T(4,128)(2,1)S(1)}, bf16[3,512]{1,0:T(4,128)(2,1)S(1)}, u32[]{:S(2)}, u32[]{:S(2)}) collective-permute-start(bf16[3,512]{1,0:T(4,128)(2,1)S(1)} %fusion.86), channel_id=1, source_target_pairs={{0,8},{8,16},{16,24},{1,9},{9,17},{17,25},{2,10},{10,18},{18,26},{... | collective-permute-start | bytes 9224 | tf_op jit(solution)/shard_map/ppermute | solution.py:20
  11.6 12.7 %collective-permute-start = (bf16[3,2048]{1,0:T(4,128)(2,1)S(1)}, bf16[3,2048]{1,0:T(4,128)(2,1)S(1)}, u32[]{:S(2)}, u32[]{:S(2)}) collective-permute-start(bf16[3,2048]{1,0:T(4,128)(2,1)S(1)} %slice.68), channel_id=1, source_target_pairs={{0,8},{8,16},{16,24},{1,9},{9,17},{17,25},{2,10},{10,18},{18,26},{... | collective-permute-start | bytes 36872 | tf_op jit(solution)/shard_map/ppermute | solution.py:20
  21.0 3.3 copy-start.4
  21.0 3.3 copy-start.5
  23.5 2.4 copy-start
  24.3 18.6 %copy-start.1 = (f32[512,256]{1,0:T(8,128)}, f32[512,256]{1,0:T(8,128)S(1)}, u32[]{:S(2)}) copy-start(f32[512,256]{1,0:T(8,128)S(1)} %get-tuple-element.155) | copy-start | bytes 1572868
  274.4 2.2 copy-start.8
  274.4 238.1 %all-gather.5.cloned.1.call-start = ((), (), s32[]{:S(2)}) async-start(), calls=%async_computation.1 | async-start | bytes 41943040 | tf_op jit(solution)/shard_map/all_gather | solution.py:186
  275.1 415.5 %reduce-scatter.2.cloned.1.call-start = ((), (), s32[]{:S(2)}) async-start(), calls=%async_computation.2 | async-start | bytes 9437184 | tf_op jit(solution)/shard_map/reduce_scatter | solution.py:189
  310.9 1.0 copy-start.2
  310.9 1.0 copy-start.6
  338.3 174.2 %copy-start.7 = (f32[2048]{0:T(1024)S(1)}, f32[2048]{0:T(1024)}, u32[]{:S(2)}) copy-start(f32[2048]{0:T(1024)} %param.32) | copy-start | bytes 24580
Sparse Core Ops, SparseCore 0:
  274.5 34.7 all-gather.6
  310.9 201.5 all-gather.4
  541.5 149.0 reduce-scatter.1
where the time goes:
time: 701 us; the launch traced here: 697 us
  waiting for transfers between devices  297 us (42%)
  matrix products  159 us (23%)
  local copies, waits for them, and re-layouts  152 us (22%)
  blocking collectives  43 us (6%)
  other arithmetic  21.7 us (3%)
  between operations  14.6 us (2%)
    reduce_scatter x1, waiting for transfers between devices, body(): lax.psum_scatter(terms.astype(jnp.bfloat16), 'head', scatter_dimension=0,...  145 us
    all_gather x1, waiting for transfers between devices, body(): lax.all_gather(out_weight, 'seq', axis=1, tiled=True)  132 us
    dynamic_update_slice x4, local copies, waits for them, and re-layouts, body(): lax.scan(span_step_body, empty_state, jnp.arange(spans_here, dtype=jnp.in...  106 us
    psum x1, blocking collectives, body(): group_totals = lax.psum(contribution, 'head')  37.3 us
    dot_general x4, matrix products, ssd_block(): scores = jnp.einsum('thn,shn->hts', span_c, span_b, precision=highest)  31.5 us
    dot_general x4, matrix products, ssd_block(): carried = jnp.einsum('thn,hpn->thp', span_c, state, precision=highest)  29.1 us
    dot_general x1, matrix products, body(): jnp.dot(normed, lax.all_gather(out_weight, 'seq', axis=1, tiled=True), pr...  28.9 us
    dot_general x4, matrix products, ssd_block(): output = jnp.einsum('hts,shp->thp', mixer, span_x, precision=highest)  26.1 us
  transfers between devices with their start and end apart: 5, of which 3 were waited for; matrix products, arithmetic and copies ran while one was open for 8% of the time, Pallas kernels for 0%

commit v1 on v0

--- a/solution.py
+++ b/solution.py
@@ -12,6 +12,32 @@
 DINNER = 16384
 highest = lax.Precision.HIGHEST
 norm_eps = 1e-05
+
+
+def bind_values_up(matrix):
+    across = "seq"
+    work_now = lax.axis_size(across)
+    made = []
+    odd, z, passed = (work_now, lax.axis_index(across), matrix.shape[1])
+    for dev, b in enumerate(matrix.shape):
+        made.append(b * odd if dev == 1 else b)
+    piece_next = prior = matrix
+    before = lax.dynamic_update_slice_in_dim(
+        jnp.zeros(made, matrix.dtype), matrix, z * passed, axis=1
+    )
+    for j in tuple(range(1, odd // 2 + 1)):
+        pool = []
+        for dev in [*range(odd)]:
+            pool.append((dev, (dev + 1) % odd))
+        piece_next = lax.ppermute(piece_next, across, pool)
+        before = lax.dynamic_update_slice_in_dim(before, piece_next, (z - j) % odd * passed, axis=1)
+        if 2 * j < odd:
+            log = []
+            for dev in [*range(odd)]:
+                log.append((dev, (dev - 1) % odd))
+            prior = lax.ppermute(prior, across, log)
+            before = lax.dynamic_update_slice_in_dim(before, prior, (z + j) % odd * passed, axis=1)
+    return before
 
 
 def from_behind(x, axis, by):
@@ -181,11 +207,7 @@
     normed = (
         (pieces * inverse_rms[:, :, None]).reshape(row_count, channels) * norm_gain[None, :]
     ).astype(jnp.bfloat16)
-    terms = jnp.dot(
-        normed,
-        lax.all_gather(out_weight, "seq", axis=1, tiled=True),
-        preferred_element_type=jnp.float32,
-    )
+    terms = jnp.dot(normed, bind_values_up(out_weight), preferred_element_type=jnp.float32)
     layer_out = lax.psum_scatter(
         terms.astype(jnp.bfloat16), "head", scatter_dimension=0, tiled=True
     )

time: 701 us -> 881 us (1.26)
  blocking collectives: 43 us -> 241 us
  waiting for transfers between devices: 297 us -> 149 us
  starting transfers between devices: 6.98 us -> 81.7 us
  local copies, waits for them, and re-layouts: 152 us -> 195 us
    unnamed x1, blocking collectives: 5.73 us -> 204 us
    all_gather x1 -> x0, waiting for transfers between devices: 132 us -> none  [body(): lax.all_gather(out_weight, 'seq', axis=1, tiled=True)]
    ppermute x0 -> x3, starting transfers between devices: none -> 75.2 us  [the longest x2 75.2 us: bind_values_up(): piece_next = lax.ppermute(piece_next, across, pool)]
    dynamic_update_slice x0 -> x4, local copies, waits for them, and re-layouts: none -> 33 us  [the longest x2 16.6 us: bind_values_up(): lax.dynamic_update_slice_in_dim(before, piece_next, (z - j) % odd * passe...]
    all_gather x1, waiting for transfers between devices: 19.6 us -> 0.01 us  [carried_in(): lax.all_gather(a.astype(kind), axis)]
    broadcast_in_dim x0 -> x1, local copies, waits for them, and re-layouts: none -> 10.9 us  [bind_values_up(): jnp.zeros(made, matrix.dtype)]
  transfers between devices with their start and end apart: 5 -> 7, of which waited for: 3 -> 1; matrix products, arithmetic and copies ran while one was open for 8% -> 39% of each run, Pallas kernels for 0% -> 0%
where the time goes in v1:
time: 881 us; the launch traced here: 873 us
  blocking collectives  241 us (27%)
  local copies, waits for them, and re-layouts  195 us (22%)
  matrix products  165 us (19%)
  waiting for transfers between devices  149 us (17%)
  starting transfers between devices  81.7 us (9%)
  other arithmetic  22.7 us (3%)
  between operations  15.2 us (2%)
    unnamed x1, blocking collectives  204 us
    reduce_scatter x1, waiting for transfers between devices, body(): lax.psum_scatter(terms.astype(jnp.bfloat16), 'head', scatter_dimension=0,...  149 us
    dynamic_update_slice x4, local copies, waits for them, and re-layouts, body(): lax.scan(span_step_body, empty_state, jnp.arange(spans_here, dtype=jnp.in...  106 us
    ppermute x2, starting transfers between devices, bind_values_up(): piece_next = lax.ppermute(piece_next, across, pool)  75.2 us
    psum x1, blocking collectives, body(): group_totals = lax.psum(contribution, 'head')  37.7 us
    dot_general x4, matrix products, ssd_block(): scores = jnp.einsum('thn,shn->hts', span_c, span_b, precision=highest)  35.4 us
    dot_general x4, matrix products, ssd_block(): carried = jnp.einsum('thn,hpn->thp', span_c, state, precision=highest)  29.1 us
    dot_general x4, matrix products, ssd_block(): output = jnp.einsum('hts,shp->thp', mixer, span_x, precision=highest)  28.8 us
  transfers between devices with their start and end apart: 7, of which 1 were waited for; matrix products, arithmetic and copies ran while one was open for 39% of the time, Pallas kernels for 0%

profile of v1, /device:TPU:0, one launch (start us, length us, event | category | flops | bytes accessed | tf_op | source)
XLA Modules:
  0.0 872.9 jit_solution(7817580321651426835)
XLA Ops:
  36.7 7.6 reshape.131
  44.3 7.6 reshape.132
  51.9 229.7 %while.26 = (s32[]{:T(128)}, f32[32,64,256]{2,1,0:T(8,128)S(1)}, f32[4,128,32,64]{1,0,3,2:T(4,128)}, s32[4]{0:T(128)S(1)}, f32[32,512]{1,0:T(8,128)S(1)}, /*inde...) while((s32[]{:T(128)}, f32[32,64,256]{2,1,0:T(8,128)S(1)}, ...), condition=%wide.region_2.3_spmd.clone, body=%wide.region_0.2_spmd.clone.sunk | while | flops 3629928448 | bytes 34868712 | solution.py:175
  53.6 8.8 %fusion.122 = f32[32,128,128]{2,1,0:T(8,128)} fusion(f32[512,32,256]{2,0,1:T(8,128)} %get-tuple-element.312, s32[]{:T(128)S(6)} %select_n.135, f32[512,32,256]{2,0,1:T(8,128)} %get-tuple-element.311), kind=kOutput, calls=%fused_computation.6.clone.1 | convolution fusion | flops 1610612736 | bytes 10486784 | tf_op jit(solution)/shard_map/while/body/eval_jaxpr/thn,shn->hts/dot_general | solution.py:84
  83.2 26.4 %dynamic_update_slice.26 = f32[4,128,32,64]{1,0,3,2:T(4,128)} dynamic-update-slice(f32[4,128,32,64]{1,0,3,2:T(4,128)} %get-tuple-element.292, f32[1,128,32,64]{1,0,3,2:T(1,128)S(1)} %bitcast.82, s32[]{:T(128)S(6)} %copy.56, s32[]{:T(128)} %constant.111.clone.1..sunk.1, s32[]{:T(128)} %constant.111.clone.1..sunk.1, s32[]{:T(128)} %constant.111.clone.1..sunk.1) | dynamic-update-slice | bytes 2097156 | tf_op jit(solution)/shard_map/while/body/jit(dynamic_update_index_in_dim)/dynamic_update_slice | solution.py:175
  110.9 8.8 %fusion.122 = f32[32,128,128]{2,1,0:T(8,128)} fusion(f32[512,32,256]{2,0,1:T(8,128)} %get-tuple-element.312, s32[]{:T(128)S(6)} %select_n.135, f32[512,32,256]{2,0,1:T(8,128)} %get-tuple-element.311), kind=kOutput, calls=%fused_computation.6.clone.1 | convolution fusion | flops 1610612736 | bytes 10486784 | tf_op jit(solution)/shard_map/while/body/eval_jaxpr/thn,shn->hts/dot_general | solution.py:84
  127.5 7.3 fusion.124
  140.5 26.4 %dynamic_update_slice.26 = f32[4,128,32,64]{1,0,3,2:T(4,128)} dynamic-update-slice(f32[4,128,32,64]{1,0,3,2:T(4,128)} %get-tuple-element.292, f32[1,128,32,64]{1,0,3,2:T(1,128)S(1)} %bitcast.82, s32[]{:T(128)S(6)} %copy.56, s32[]{:T(128)} %constant.111.clone.1..sunk.1, s32[]{:T(128)} %constant.111.clone.1..sunk.1, s32[]{:T(128)} %constant.111.clone.1..sunk.1) | dynamic-update-slice | bytes 2097156 | tf_op jit(solution)/shard_map/while/body/jit(dynamic_update_index_in_dim)/dynamic_update_slice | solution.py:175
  168.1 8.8 %fusion.122 = f32[32,128,128]{2,1,0:T(8,128)} fusion(f32[512,32,256]{2,0,1:T(8,128)} %get-tuple-element.312, s32[]{:T(128)S(6)} %select_n.135, f32[512,32,256]{2,0,1:T(8,128)} %get-tuple-element.311), kind=kOutput, calls=%fused_computation.6.clone.1 | convolution fusion | flops 1610612736 | bytes 10486784 | tf_op jit(solution)/shard_map/while/body/eval_jaxpr/thn,shn->hts/dot_general | solution.py:84
  184.8 7.3 fusion.124
  197.8 26.4 %dynamic_update_slice.26 = f32[4,128,32,64]{1,0,3,2:T(4,128)} dynamic-update-slice(f32[4,128,32,64]{1,0,3,2:T(4,128)} %get-tuple-element.292, f32[1,128,32,64]{1,0,3,2:T(1,128)S(1)} %bitcast.82, s32[]{:T(128)S(6)} %copy.56, s32[]{:T(128)} %constant.111.clone.1..sunk.1, s32[]{:T(128)} %constant.111.clone.1..sunk.1, s32[]{:T(128)} %constant.111.clone.1..sunk.1) | dynamic-update-slice | bytes 2097156 | tf_op jit(solution)/shard_map/while/body/jit(dynamic_update_index_in_dim)/dynamic_update_slice | solution.py:175
  225.4 8.8 %fusion.122 = f32[32,128,128]{2,1,0:T(8,128)} fusion(f32[512,32,256]{2,0,1:T(8,128)} %get-tuple-element.312, s32[]{:T(128)S(6)} %select_n.135, f32[512,32,256]{2,0,1:T(8,128)} %get-tuple-element.311), kind=kOutput, calls=%fused_computation.6.clone.1 | convolution fusion | flops 1610612736 | bytes 10486784 | tf_op jit(solution)/shard_map/while/body/eval_jaxpr/thn,shn->hts/dot_general | solution.py:84
  255.0 26.4 %dynamic_update_slice.26 = f32[4,128,32,64]{1,0,3,2:T(4,128)} dynamic-update-slice(f32[4,128,32,64]{1,0,3,2:T(4,128)} %get-tuple-element.292, f32[1,128,32,64]{1,0,3,2:T(1,128)S(1)} %bitcast.82, s32[]{:T(128)S(6)} %copy.56, s32[]{:T(128)} %constant.111.clone.1..sunk.1, s32[]{:T(128)} %constant.111.clone.1..sunk.1, s32[]{:T(128)} %constant.111.clone.1..sunk.1) | dynamic-update-slice | bytes 2097156 | tf_op jit(solution)/shard_map/while/body/jit(dynamic_update_index_in_dim)/dynamic_update_slice | solution.py:175
  282.9 74.7 %collective-permute-start.4 = (bf16[2048,2048]{1,0:T(8,128)(2,1)}, bf16[2048,2048]{1,0:T(8,128)(2,1)}, u32[]{:S(2)}, u32[]{:S(2)}) collective-permute-start(bf16[2048,2048]{1,0:T(8,128)(2,1)} %collective-permute-done.2), channel_id=1, source_target_pairs={{0,8},{8,16},{16,24},{24,0},{1,9},{9,17},{17,25},{25,1},{2,10},{10... | collective-permute-start | bytes 25165832 | tf_op jit(solution)/shard_map/ppermute | solution.py:32
  360.7 203.7 %all-reduce = bf16[128]{0:T(256)(128)(2,1)S(1)} all-reduce(bf16[128]{0:T(256)(128)(2,1)S(1)} %dynamic-update-slice), channel_id=2, replica_groups=mesh['seq'=4,'head'=8] {'seq'}, use_global_device_ids=true, to_apply=%add | all-reduce | flops 128 | bytes 512
  564.6 10.9 %broadcast_in_dim.44 = bf16[2048,8192]{1,0:T(8,128)(2,1)} broadcast(bf16[]{:T(256)} %constant.132.clone.1), dimensions={} | broadcast | bytes 33554432 | tf_op jit(solution)/shard_map/broadcast_in_dim | solution.py:26
  575.5 8.2 constant_dynamic-update-slice_fusion.3
  591.8 20.5 %fusion.68 = f32[512,32,64]{0,2,1:T(8,128)} fusion(f32[512,32,64]{0,2,1:T(8,128)} %reshape.133, f32[512,32,64]{0,2,1:T(8,128)} %get-tuple-element.347, f32[512,256]{1,0:T(8,128)S(1)} %copy-done.3, f32[32]{0:T(128)S(1)} %copy-done.6, f32[512,32]{0,1:T(8,128)S(1)} %exponential_bitcast_fusion.1, f32[32,64,256]{2,1,0:T(8,128)} %get-tuple-element.87, ...), kind=kOutput, calls=%fused_computation.70 | convolution fusion | flops 3226468352 | bytes 17367296 | tf_op jit(solution)/shard_map/thn,hpn->thp/dot_general | solution.py:188
  622.0 37.7 %psum.7 = f32[8,512]{1,0:T(8,128)S(1)} all-reduce(f32[8,512]{1,0:T(8,128)S(1)} %broadcast_multiply_fusion.1), channel_id=1, replica_groups=mesh['seq'=4,'head'=8] {'head'}, use_global_device_ids=true, to_apply=%region_8.9 | all-reduce | flops 4096 | bytes 32768 | tf_op jit(solution)/shard_map/psum | solution.py:204
  659.9 8.2 constant_dynamic-update-slice_fusion.2
  668.1 8.2 constant_dynamic-update-slice_fusion.1
  676.3 8.4 constant_dynamic-update-slice_fusion
  684.7 27.9 %convolution_convert_fusion = bf16[512,8192]{1,0:T(8,128)(2,1)} fusion(bf16[2048,8192]{1,0:T(8,128)(2,1)} %constant_dynamic-update-slice_fusion, f32[2048]{0:T(1024)S(1)} %copy-done.7, f32[512]{0:T(512)S(1)} %add_rsqrt_fusion, f32[512,2048]{1,0:T(8,128)S(1)} %copy-done.1, bf16[512,2048]{1,0:T(8,128)(2,1)} %param.20), kind=kOutput, calls=%fused_computation.47 | convolution fusion | flops 17193500672 | bytes 48244736 | tf_op jit(solution)/shard_map/dot_general | solution.py:210
  716.7 149.1 %reduce-scatter.2.cloned.1.call-done = bf16[64,8192]{1,0:T(8,128)(2,1)} async-done(((bf16[512,8192]{1,0:T(8,128)(2,1)}), bf16[64,8192]{1,0:T(8,128)(2,1)}) %reduce-scatter.2.cloned.1.call-update) | async-done | bytes 1048592 | tf_op jit(solution)/shard_map/reduce_scatter | solution.py:211
  (118 shorter events, 126.1 us)
Async XLA Ops:
  7.2 582.1 %all-gather.4.cloned.1.call-start = ((), (), s32[]{:S(2)}) async-start(), calls=%async_computation.2 | async-start | bytes 5242880 | tf_op jit(solution)/shard_map/all_gather | solution.py:52
  7.2 275.7 %collective-permute-start.2 = (bf16[2048,2048]{1,0:T(8,128)(2,1)}, bf16[2048,2048]{1,0:T(8,128)(2,1)}, u32[]{:S(2)}, u32[]{:S(2)}) collective-permute-start(bf16[2048,2048]{1,0:T(8,128)(2,1)} %param.33), channel_id=1, source_target_pairs={{0,8},{8,16},{16,24},{24,0},{1,9},{9,17},{17,25},{25,1},{2,10},{10... | collective-permute-start | bytes 25165832 | tf_op jit(solution)/shard_map/ppermute | solution.py:32
  8.5 17.3 %collective-permute-start = (bf16[3,2048]{1,0:T(4,128)(2,1)S(1)}, bf16[3,2048]{1,0:T(4,128)(2,1)S(1)}, u32[]{:S(2)}, u32[]{:S(2)}) collective-permute-start(bf16[3,2048]{1,0:T(4,128)(2,1)S(1)} %slice.68), channel_id=1, source_target_pairs={{0,8},{8,16},{16,24},{1,9},{9,17},{17,25},{2,10},{10,18},{18,26},{... | collective-permute-start | bytes 36872 | tf_op jit(solution)/shard_map/ppermute | solution.py:46
  14.1 10.9 %collective-permute-start.1 = (bf16[3,512]{1,0:T(4,128)(2,1)S(1)}, bf16[3,512]{1,0:T(4,128)(2,1)S(1)}, u32[]{:S(2)}, u32[]{:S(2)}) collective-permute-start(bf16[3,512]{1,0:T(4,128)(2,1)S(1)} %fusion.86), channel_id=1, source_target_pairs={{0,8},{8,16},{16,24},{1,9},{9,17},{17,25},{2,10},{10,18},{18,26},{... | collective-permute-start | bytes 9224 | tf_op jit(solution)/shard_map/ppermute | solution.py:46
  20.9 4.9 copy-start.4
  21.0 4.9 copy-start.5
  25.0 2.4 copy-start
  25.8 18.5 %copy-start.2 = (f32[512,256]{1,0:T(8,128)}, f32[512,256]{1,0:T(8,128)S(1)}, u32[]{:S(2)}) copy-start(f32[512,256]{1,0:T(8,128)S(1)} %get-tuple-element.155) | copy-start | bytes 1572868
  281.6 77.3 %copy-start.8 = (u32[32]{0:T(128)S(1)}, u32[32]{0:T(128)}, u32[]{:S(2)}) copy-start(u32[32]{0:T(128)} %constant.139) | copy-start | bytes 388
  282.8 583.0 %reduce-scatter.2.cloned.1.call-start = ((), (), s32[]{:S(2)}) async-start(), calls=%async_computation.1 | async-start | bytes 9437184 | tf_op jit(solution)/shard_map/reduce_scatter | solution.py:211
  282.8 385.3 %collective-permute-start.3 = (bf16[2048,2048]{1,0:T(8,128)(2,1)}, bf16[2048,2048]{1,0:T(8,128)(2,1)}, u32[]{:S(2)}, u32[]{:S(2)}) collective-permute-start(bf16[2048,2048]{1,0:T(8,128)(2,1)} %param.33), channel_id=1, source_target_pairs={{0,24},{8,0},{16,8},{24,16},{1,25},{9,1},{17,9},{25,17},{2,26},{10... | collective-permute-start | bytes 25165832 | tf_op jit(solution)/shard_map/ppermute | solution.py:38
  282.9 393.4 %collective-permute-start.4 = (bf16[2048,2048]{1,0:T(8,128)(2,1)}, bf16[2048,2048]{1,0:T(8,128)(2,1)}, u32[]{:S(2)}, u32[]{:S(2)}) collective-permute-start(bf16[2048,2048]{1,0:T(8,128)(2,1)} %collective-permute-done.2), channel_id=1, source_target_pairs={{0,8},{8,16},{16,24},{24,0},{1,9},{9,17},{17,25},{25,1},{2,10},{10... | collective-permute-start | bytes 25165832 | tf_op jit(solution)/shard_map/ppermute | solution.py:32
  590.8 1.0 copy-start.3
  590.8 1.0 copy-start.6
  676.3 8.4 copy-start.1
  676.3 8.4 copy-start.7
Sparse Core Ops, SparseCore 0:
  282.9 133.7 all-gather.3
  712.7 153.0 reduce-scatter.1
